TPU v7x, 32 devices: a whole 2x2x4 slice. The times are simulated.
32 devices in a mesh: tgt: 8 (over z, core), src: 4 (over y, x).
Axes of the slice: x: 2, y: 2, z: 4, core: 2. Of those that a mesh axis runs over, the one named last changes fastest.
Arguments:
- right_side: float32 [8192], P(('tgt', 'src')), may hold values from -50 to 50
- targets: float32 [3, 8192], P(None, ('tgt', 'src')), may hold values from -1 to 1
- source_nodes: float32 [3, 16, 8192], P(None, None, ('tgt', 'src')), may hold values from -1 to 1
- node_weights: float32 [16, 8192], P(None, ('tgt', 'src')), may hold values from -0.02734375 to 0.02734375
- near_list: int32 [2, 384], P(None, ('tgt', 'src')), may hold values from 0 to 31, as said below
- near_count: int32 [32], P(('tgt', 'src')), may hold values from 1 to 12, as said below
- row_basis: float32 [32, 32, 256], P(('tgt', 'src')), may hold values from -1 to 1
- column_basis: float32 [32, 32, 256], P(('tgt', 'src')), may hold values from -0.375 to 0.375
- coupling: float32 [8, 4, 8, 4, 1024], P('tgt', None, None, 'src'), may hold values from -0.109375 to 0.109375
Outputs:
- solution: float32 [8192], P(('tgt', 'src'))
Inputs may be any that keep to these rules, and one draw needn't show every extreme that they name: `near_list`: for the device with tgt index i and src index j (slots j + i * 4 times 12 onward), every slot names a target cluster c with c // 4 = i and a source cluster d with d % 4 = j; the slots of one device name distinct pairs. `near_count`: some device has all 12 slots live.
All inputs are finite; a program needn't handle non-finite values.
Results may differ from a plain program's by a relative error of at most 0.0003.
Values sent between devices are 32-bit elements; how exact they have to be, the bound alone decides.
No kernel may reach another device: no remote copies, remote signals or barrier semaphores. Data moves between devices by JAX's collectives and lax.ppermute only.
A program may use at most 64 MiB of HBM per device.

v0:
```python
import jax
import jax.numpy as jnp
from jax import lax
from jax.sharding import PartitionSpec as P

spread_sq = 0.0004
norm_floor = 1e-06
highest = lax.Precision.HIGHEST


def tile_values(points, src_nodes, src_weights):
    summed = jnp.zeros((points.shape[1], src_nodes.shape[2]), jnp.float32)
    for node_index in range(src_nodes.shape[1]):
        offset_first = points[0][:, None] - src_nodes[0, node_index][None, :]
        offset_second = points[1][:, None] - src_nodes[1, node_index][None, :]
        offset_third = points[2][:, None] - src_nodes[2, node_index][None, :]
        distance = jnp.sqrt(
            offset_first * offset_first
            + offset_second * offset_second
            + offset_third * offset_third
            + spread_sq
        )
        summed = summed + src_weights[node_index][None, :] / distance
    return summed


def global_sum(value):
    return lax.psum(value, ("tgt", "src"))


def per_device(
    right_side,
    targets,
    source_nodes,
    node_weights,
    near_list,
    near_count,
    row_basis,
    column_basis,
    coupling,
):
    src_count = lax.axis_size("src")
    tgt_count = lax.axis_size("tgt")
    tgt_index = lax.axis_index("tgt")
    leaf_size = right_side.shape[0]
    slot_total = near_list.shape[1]
    rank_size = row_basis.shape[1]
    slot_ids = jnp.arange(slot_total, dtype=jnp.int32)
    live_slot = slot_ids < near_count[0]
    row_local = near_list[0] - tgt_index * src_count
    column_local = near_list[1] // src_count
    row_hits = (
        (row_local[:, None] == jnp.arange(src_count, dtype=jnp.int32)[None, :]) & live_slot[:, None]
    ).astype(jnp.float32)
    column_hits = (column_local[:, None] == jnp.arange(tgt_count, dtype=jnp.int32)[None, :]).astype(
        jnp.float32
    )
    near_mask = jnp.einsum("ka,kb->ab", row_hits, column_hits, precision=highest)
    coupled = (
        coupling.reshape(src_count, tgt_count, rank_size, rank_size)
        * (1.0 - near_mask)[:, :, None, None]
    )
    row_points = lax.all_gather(targets, "src", axis=1, tiled=True)
    row_blocks = row_points.reshape(3, src_count, leaf_size)
    row_bases = lax.all_gather(row_basis, "src", axis=0, tiled=True)
    node_rows, weight_rows = (
        lax.all_gather(source_nodes[None], "tgt", axis=0, tiled=True),
        lax.all_gather(node_weights[None], "tgt", axis=0, tiled=True),
    )

    def make_tile(slot_number):

        def compute(unused):
            return tile_values(
                row_blocks[:, row_local[slot_number]],
                node_rows[column_local[slot_number]],
                weight_rows[column_local[slot_number]],
            )

        def nothing(unused):
            return jnp.zeros((leaf_size, leaf_size), jnp.float32)

        return lax.cond(live_slot[slot_number], compute, nothing, 0)

    tile_cache = lax.map(make_tile, slot_ids)

    def operate(vector):
        coeffs = jnp.dot(column_basis[0], vector, precision=highest)
        value_rows, coeff_rows = (
            lax.all_gather(vector[None], "tgt", axis=0, tiled=True),
            lax.all_gather(coeffs[None], "tgt", axis=0, tiled=True),
        )
        selected = value_rows[column_local]
        contrib = jnp.einsum("kij,kj->ki", tile_cache, selected, precision=highest)
        near_rows = jnp.einsum("ka,ki->ai", row_hits, contrib, precision=highest)
        far_rows = jnp.einsum("abrs,bs->ar", coupled, coeff_rows, precision=highest)
        partial_rows = near_rows + jnp.einsum("ar,arp->ap", far_rows, row_bases, precision=highest)
        own_rows = lax.psum_scatter(partial_rows, "src", scatter_dimension=0, tiled=True)
        result = own_rows[0]
        return 0.5 * vector + result

    rhs_norm = jnp.sqrt(global_sum(jnp.sum(right_side * right_side)) + norm_floor)
    basis_one = right_side / rhs_norm
    image_one = operate(basis_one)
    proj_first = global_sum(jnp.sum(basis_one * image_one))
    rest_one = image_one - proj_first * basis_one
    height_first = jnp.sqrt(global_sum(jnp.sum(rest_one * rest_one)) + norm_floor)
    basis_two = rest_one / height_first
    image_two = operate(basis_two)
    proj_cross = global_sum(jnp.sum(basis_one * image_two))
    rest_two = image_two - proj_cross * basis_one
    proj_second = global_sum(jnp.sum(basis_two * rest_two))
    rest_two = rest_two - proj_second * basis_two
    height_second = jnp.sqrt(global_sum(jnp.sum(rest_two * rest_two)) + norm_floor)
    radius_first = jnp.sqrt(proj_first * proj_first + height_first * height_first)
    cos_first = proj_first / radius_first
    sin_first = height_first / radius_first
    rotated_top = cos_first * proj_cross + sin_first * proj_second
    rotated_low = cos_first * proj_second - sin_first * proj_cross
    radius_second = jnp.sqrt(rotated_low * rotated_low + height_second * height_second)
    coeff_second = -sin_first * rhs_norm * (rotated_low / radius_second) / radius_second
    coeff_first = (cos_first * rhs_norm - rotated_top * coeff_second) / radius_first
    return coeff_first * basis_one + coeff_second * basis_two


def solution(mesh):
    return jax.shard_map(
        per_device,
        mesh=mesh,
        in_specs=(
            P(("tgt", "src")),
            P(None, ("tgt", "src")),
            P(None, None, ("tgt", "src")),
            P(None, ("tgt", "src")),
            P(None, ("tgt", "src")),
            P(("tgt", "src")),
            P(("tgt", "src"), None, None),
            P(("tgt", "src"), None, None),
            P("tgt", None, None, "src", None),
        ),
        out_specs=P(("tgt", "src")),
        check_vma=False,
    )
```

profile of v0, /device:TPU:0, one launch (start us, length us, event | category | flops | bytes accessed | tf_op | source)
XLA Modules:
  0.0 570.8 jit_solution(8423042894770920571)
XLA Ops:
  1.4 17.0 %all-gather = f32[128,256]{1,0:T(8,128)} all-gather(f32[16,256]{1,0:T(8,128)} %param.16), channel_id=2, replica_groups=mesh['tgt'=8,'src'=4] {'tgt'}, dimensions={0}, use_global_device_ids=true | all-gather | bytes 147456 | tf_op jit(solution)/shard_map/all_gather | solution.py:68
  19.1 8.3 %all_gather.25 = f32[3,1024]{1,0:T(4,128)S(1)} all-gather(f32[3,256]{1,0:T(4,128)} %param.14), channel_id=1, replica_groups=mesh['tgt'=8,'src'=4] {'src'}, dimensions={1}, use_global_device_ids=true | all-gather | bytes 15360 | tf_op jit(solution)/shard_map/all_gather | solution.py:63
  27.4 15.8 %all-gather.1 = f32[24,16,256]{2,1,0:T(8,128)} all-gather(f32[3,16,256]{2,1,0:T(8,128)} %param.15), channel_id=3, replica_groups=mesh['tgt'=8,'src'=4] {'tgt'}, dimensions={0}, use_global_device_ids=true | all-gather | bytes 442368 | tf_op jit(solution)/shard_map/all_gather | solution.py:67
  43.2 71.8 %while.10 = (s32[]{:T(128)}, f32[12,256,256]{2,1,0:T(8,128)S(1)}, s32[12]{0:T(128)S(1)}, pred[12]{0:T(512)(128)(4,1)S(1)}, s32[12]{0:T(128)S(1)}, /*index=5*/f32...) while((s32[]{:T(128)}, f32[12,256,256]{2,1,0:T(8,128)S(1)}, ...), condition=%wide.region_5.6_spmd, body=%wide.region_2.0_spmd.sunk | while | flops 11468830 | bytes 1091180 | solution.py:85
  47.3 11.1 %conditional.2 = (f32[1,256,256]{2,1,0:T(8,128)S(1)}) conditional(s32[]{:T(128)} %bitcast.164, () %tuple.106, (s32[]{:T(128)}, s32[12]{0:T(128)S(1)}, f32[8,16,256]{2,1,0:T(8,128)}, s32[12]{0:T(128)S(1)}, f32[3,4,256]{2,1,0:T(4,128)S(1)}, /*index=5*/f32[8,3,16,256]{3,2,1,0:T(8,128)}) %tuple.107), branch_computations={%region_3.3_spmd, %region_4.4_spmd} | conditional | flops 11468824 | bytes 566658 | solution.py:83
  51.9 0.8 dynamic-slice_bitcast_fusion
  55.3 1.1 constant_dynamic-slice_fusion.15
  56.5 1.9 multiply_add_fusion
  62.5 11.1 %conditional.2 = (f32[1,256,256]{2,1,0:T(8,128)S(1)}) conditional(s32[]{:T(128)} %bitcast.164, () %tuple.106, (s32[]{:T(128)}, s32[12]{0:T(128)S(1)}, f32[8,16,256]{2,1,0:T(8,128)}, s32[12]{0:T(128)S(1)}, f32[3,4,256]{2,1,0:T(4,128)S(1)}, /*index=5*/f32[8,3,16,256]{3,2,1,0:T(8,128)}) %tuple.107), branch_computations={%region_3.3_spmd, %region_4.4_spmd} | conditional | flops 11468824 | bytes 566658 | solution.py:83
  70.6 1.1 constant_dynamic-slice_fusion.15
  71.7 1.9 multiply_add_fusion
  115.7 148.2 %psum.42 = f32[]{:T(128)} all-reduce(f32[]{:T(128)} %multiply_reduce_fusion.5), channel_id=1, replica_groups=mesh['tgt'=8,'src'=4] {'tgt','src'}, use_global_device_ids=true, to_apply=%region_1.2 | all-reduce | flops 1 | bytes 8 | tf_op jit(solution)/shard_map/psum | solution.py:28
  264.7 10.7 %all-gather.6 = f32[8,1,256]{2,1,0:T(1,128)S(1)} all-gather(f32[1,1,256]{2,1,0:T(1,128)S(1)} %bitcast.249), channel_id=4, replica_groups=mesh['tgt'=8,'src'=4] {'tgt'}, dimensions={0}, use_global_device_ids=true | all-gather | bytes 9216 | tf_op jit(solution)/shard_map/all_gather | solution.py:90
  276.0 2.7 fusion.12
  280.4 13.9 %all-reduce = f32[256]{0:T(256)S(1)} all-reduce(f32[256]{0:T(256)S(1)} %dynamic-update-slice), channel_id=5, replica_groups=mesh['tgt'=8,'src'=4] {'tgt'}, use_global_device_ids=true, to_apply=%add | all-reduce | flops 256 | bytes 2048
  294.7 1.0 reshape.2740
  295.9 2.2 convolution_bitcast_fusion.1
  298.1 9.4 %all_gather.29 = f32[4,32,256]{2,1,0:T(8,128)S(1)} all-gather(f32[1,32,256]{2,1,0:T(8,128)S(1)} %copy-done.3), channel_id=1, replica_groups=mesh['tgt'=8,'src'=4] {'src'}, dimensions={0}, use_global_device_ids=true | all-gather | bytes 163840 | tf_op jit(solution)/shard_map/all_gather | solution.py:65
  308.0 9.2 %all-reduce.2 = f32[4,256]{1,0:T(4,128)S(1)} all-reduce(f32[4,256]{1,0:T(4,128)S(1)} %convolution_add_fusion.1), channel_id=8, replica_groups=mesh['tgt'=8,'src'=4] {'src'}, use_global_device_ids=true, to_apply=%region_6.7.clone | all-reduce | flops 1024 | bytes 8192
  319.2 37.0 %psum.43 = f32[]{:T(128)} all-reduce(f32[]{:T(128)} %multiply_reduce_fusion.4), channel_id=1, replica_groups=mesh['tgt'=8,'src'=4] {'tgt','src'}, use_global_device_ids=true, to_apply=%region_8.9 | all-reduce | flops 1 | bytes 8 | tf_op jit(solution)/shard_map/psum | solution.py:28
  356.2 1.2 multiply_reduce_fusion.3
  357.4 42.6 %psum.44 = f32[]{:T(128)} all-reduce(f32[]{:T(128)} %multiply_reduce_fusion.3), channel_id=1, replica_groups=mesh['tgt'=8,'src'=4] {'tgt','src'}, use_global_device_ids=true, to_apply=%region_10.11 | all-reduce | flops 1 | bytes 8 | tf_op jit(solution)/shard_map/psum | solution.py:28
  403.1 10.1 %all-gather.7 = f32[8,1,256]{2,1,0:T(1,128)S(1)} all-gather(f32[1,1,256]{2,1,0:T(1,128)S(1)} %bitcast.172), channel_id=6, replica_groups=mesh['tgt'=8,'src'=4] {'tgt'}, dimensions={0}, use_global_device_ids=true | all-gather | bytes 9216 | tf_op jit(solution)/shard_map/all_gather | solution.py:90
  413.8 2.7 fusion.10
  416.9 14.0 %all-reduce.1 = f32[256]{0:T(256)S(1)} all-reduce(f32[256]{0:T(256)S(1)} %dynamic-update-slice.1), channel_id=7, replica_groups=mesh['tgt'=8,'src'=4] {'tgt'}, use_global_device_ids=true, to_apply=%add.1 | all-reduce | flops 256 | bytes 2048
  431.0 2.2 convolution_bitcast_fusion
  433.7 10.0 %all-reduce.3 = f32[4,256]{1,0:T(4,128)S(1)} all-reduce(f32[4,256]{1,0:T(4,128)S(1)} %convolution_add_fusion), channel_id=9, replica_groups=mesh['tgt'=8,'src'=4] {'src'}, use_global_device_ids=true, to_apply=%region_11.12.clone | all-reduce | flops 1024 | bytes 8192
  445.0 37.0 %psum.45 = f32[]{:T(128)} all-reduce(f32[]{:T(128)} %multiply_reduce_fusion.2), channel_id=1, replica_groups=mesh['tgt'=8,'src'=4] {'tgt','src'}, use_global_device_ids=true, to_apply=%region_13.14 | all-reduce | flops 1 | bytes 8 | tf_op jit(solution)/shard_map/psum | solution.py:28
  482.0 1.3 multiply_reduce_fusion.1
  483.3 42.4 %psum.46 = f32[]{:T(128)} all-reduce(f32[]{:T(128)} %multiply_reduce_fusion.1), channel_id=1, replica_groups=mesh['tgt'=8,'src'=4] {'tgt','src'}, use_global_device_ids=true, to_apply=%region_15.16 | all-reduce | flops 1 | bytes 8 | tf_op jit(solution)/shard_map/psum | solution.py:28
  527.1 1.9 multiply_reduce_fusion
  529.0 39.1 %psum.47 = f32[]{:T(128)} all-reduce(f32[]{:T(128)} %multiply_reduce_fusion), channel_id=1, replica_groups=mesh['tgt'=8,'src'=4] {'tgt','src'}, use_global_device_ids=true, to_apply=%region_17.18 | all-reduce | flops 1 | bytes 8 | tf_op jit(solution)/shard_map/psum | solution.py:28
  (117 shorter events, 30.9 us)
Async XLA Ops:
  0.0 278.7 %copy-start = (f32[1,32,256]{2,1,0:T(8,128)S(1)}, f32[1,32,256]{2,1,0:T(8,128)}, u32[]{:S(2)}) copy-start(f32[1,32,256]{2,1,0:T(8,128)} %param.20) | copy-start | bytes 98308
  43.2 71.9 %copy-start.2 = (f32[256]{0:T(256)S(1)}, f32[256]{0:T(256)}, u32[]{:S(2)}) copy-start(f32[256]{0:T(256)} %param.13) | copy-start | bytes 3076
  43.2 232.1 %copy-start.4 = (s32[2,12]{1,0:T(2,128)S(1)}, s32[2,12]{1,0:T(2,128)}, u32[]{:S(2)}) copy-start(s32[2,12]{1,0:T(2,128)} %param.17) | copy-start | bytes 292
  115.1 163.8 %copy-start.6 = (u32[32]{0:T(128)S(1)}, u32[32]{0:T(128)}, u32[]{:S(2)}) copy-start(u32[32]{0:T(128)} %constant.65) | copy-start | bytes 388
  115.1 179.3 %copy-start.1 = (f32[1,4,8,1,1024]{4,3,2,1,0:T(1,128)S(1)}, f32[1,4,8,1,1024]{4,3,2,1,0:T(1,128)}, u32[]{:S(2)}) copy-start(f32[1,4,8,1,1024]{4,3,2,1,0:T(1,128)} %param.21) | copy-start | bytes 393220
  115.1 183.0 %copy-start.3 = (f32[1,32,256]{2,1,0:T(8,128)S(1)}, f32[1,32,256]{2,1,0:T(8,128)}, u32[]{:S(2)}) copy-start(f32[1,32,256]{2,1,0:T(8,128)} %param.19) | copy-start | bytes 98308
  115.1 202.1 %copy-start.5 = (u32[32]{0:T(128)S(1)}, u32[32]{0:T(128)}, u32[]{:S(2)}) copy-start(u32[32]{0:T(128)} %constant.77) | copy-start | bytes 388
where the time goes:
time: 575 us; the launch traced here: 571 us
  blocking collectives  465 us (81%)
  loops' own time  45.1 us (8%)
  local copies, waits for them, and re-layouts  28.4 us (5%)
  other arithmetic  13 us (2%)
  matrix products  11.4 us (2%)
  between operations  8.12 us (1%)
    psum x6, blocking collectives, global_sum(): return lax.psum(value, ('tgt', 'src'))  346 us
    unnamed x4, blocking collectives  47.1 us
    another operation x1, loops' own time, per_device(): tile_cache = lax.map(make_tile, slot_ids)  33 us
    all_gather x2, blocking collectives, operate(): lax.all_gather(vector[None], 'tgt', axis=0, tiled=True)  20.8 us
    all_gather x1, blocking collectives, per_device(): lax.all_gather(node_weights[None], 'tgt', axis=0, tiled=True)  17 us
    all_gather x1, blocking collectives, per_device(): lax.all_gather(source_nodes[None], 'tgt', axis=0, tiled=True)  15.8 us
    another operation x12, loops' own time, make_tile(): return lax.cond(live_slot[slot_number], compute, nothing, 0)  12.1 us

commit v1 on v0

--- a/solution.py
+++ b/solution.py
@@ -25,7 +25,7 @@
 
 
 def global_sum(value):
-    return lax.psum(value, ("tgt", "src"))
+    return lax.psum(lax.psum(value, "src"), "tgt")
 
 
 def per_device(

time: 575 us -> 477 us (0.83)
  blocking collectives: 465 us -> 367 us
    psum x6 -> x12, blocking collectives: 346 us -> 252 us  [global_sum(): return lax.psum(lax.psum(value, 'src'), 'tgt')]
where the time goes in v1:
time: 477 us; the launch traced here: 473 us
  blocking collectives  367 us (77%)
  loops' own time  45.1 us (9%)
  local copies, waits for them, and re-layouts  28.4 us (6%)
  other arithmetic  13 us (3%)
  matrix products  11.4 us (2%)
  between operations  8.12 us (2%)
    psum x12, blocking collectives, global_sum(): return lax.psum(lax.psum(value, 'src'), 'tgt')  252 us
    unnamed x4, blocking collectives  48.8 us
    another operation x1, loops' own time, per_device(): tile_cache = lax.map(make_tile, slot_ids)  33 us
    all_gather x1, blocking collectives, per_device(): lax.all_gather(node_weights[None], 'tgt', axis=0, tiled=True)  17 us
    all_gather x2, blocking collectives, operate(): lax.all_gather(vector[None], 'tgt', axis=0, tiled=True)  16.9 us
    all_gather x1, blocking collectives, per_device(): lax.all_gather(source_nodes[None], 'tgt', axis=0, tiled=True)  15.8 us
    another operation x12, loops' own time, make_tile(): return lax.cond(live_slot[slot_number], compute, nothing, 0)  12.1 us

profile of v1, /device:TPU:0, one launch (start us, length us, event | category | flops | bytes accessed | tf_op | source)
XLA Modules:
  0.0 472.8 jit_solution(10123783626653852580)
XLA Ops:
  1.4 17.0 %all-gather = f32[128,256]{1,0:T(8,128)} all-gather(f32[16,256]{1,0:T(8,128)} %param.16), channel_id=2, replica_groups=mesh['tgt'=8,'src'=4] {'tgt'}, dimensions={0}, use_global_device_ids=true | all-gather | bytes 147456 | tf_op jit(solution)/shard_map/all_gather | solution.py:68
  19.1 8.3 %all_gather.25 = f32[3,1024]{1,0:T(4,128)S(1)} all-gather(f32[3,256]{1,0:T(4,128)} %param.14), channel_id=1, replica_groups=mesh['tgt'=8,'src'=4] {'src'}, dimensions={1}, use_global_device_ids=true | all-gather | bytes 15360 | tf_op jit(solution)/shard_map/all_gather | solution.py:63
  27.4 15.8 %all-gather.1 = f32[24,16,256]{2,1,0:T(8,128)} all-gather(f32[3,16,256]{2,1,0:T(8,128)} %param.15), channel_id=3, replica_groups=mesh['tgt'=8,'src'=4] {'tgt'}, dimensions={0}, use_global_device_ids=true | all-gather | bytes 442368 | tf_op jit(solution)/shard_map/all_gather | solution.py:67
  43.2 71.8 %while.10 = (s32[]{:T(128)}, f32[12,256,256]{2,1,0:T(8,128)S(1)}, s32[12]{0:T(128)S(1)}, pred[12]{0:T(512)(128)(4,1)S(1)}, s32[12]{0:T(128)S(1)}, /*index=5*/f32...) while((s32[]{:T(128)}, f32[12,256,256]{2,1,0:T(8,128)S(1)}, ...), condition=%wide.region_6.7_spmd, body=%wide.region_3.6_spmd.sunk | while | flops 11468830 | bytes 1091180 | solution.py:85
  47.3 11.1 %conditional.2 = (f32[1,256,256]{2,1,0:T(8,128)S(1)}) conditional(s32[]{:T(128)} %bitcast.164, () %tuple.106, (s32[]{:T(128)}, s32[12]{0:T(128)S(1)}, f32[8,16,256]{2,1,0:T(8,128)}, s32[12]{0:T(128)S(1)}, f32[3,4,256]{2,1,0:T(4,128)S(1)}, /*index=5*/f32[8,3,16,256]{3,2,1,0:T(8,128)}) %tuple.107), branch_computations={%region_4.4_spmd, %region_5.5_spmd} | conditional | flops 11468824 | bytes 566658 | solution.py:83
  56.5 1.9 multiply_add_fusion
  62.5 11.1 %conditional.2 = (f32[1,256,256]{2,1,0:T(8,128)S(1)}) conditional(s32[]{:T(128)} %bitcast.164, () %tuple.106, (s32[]{:T(128)}, s32[12]{0:T(128)S(1)}, f32[8,16,256]{2,1,0:T(8,128)}, s32[12]{0:T(128)S(1)}, f32[3,4,256]{2,1,0:T(4,128)S(1)}, /*index=5*/f32[8,3,16,256]{3,2,1,0:T(8,128)}) %tuple.107), branch_computations={%region_4.4_spmd, %region_5.5_spmd} | conditional | flops 11468824 | bytes 566658 | solution.py:83
  71.7 1.9 multiply_add_fusion
  115.7 120.3 %psum.84 = f32[]{:T(128)} all-reduce(f32[]{:T(128)} %multiply_reduce_fusion.5), channel_id=1, replica_groups=mesh['tgt'=8,'src'=4] {'src'}, use_global_device_ids=true, to_apply=%region_1.2 | all-reduce | flops 1 | bytes 8 | tf_op jit(solution)/shard_map/psum | solution.py:28
  236.1 14.2 %psum.85 = f32[]{:T(128)} all-reduce(f32[]{:T(128)} %psum.84), channel_id=1, replica_groups=mesh['tgt'=8,'src'=4] {'tgt'}, use_global_device_ids=true, to_apply=%region_2.3 | all-reduce | flops 1 | bytes 8 | tf_op jit(solution)/shard_map/psum | solution.py:28
  251.0 8.4 %all-gather.6 = f32[8,1,256]{2,1,0:T(1,128)S(1)} all-gather(f32[1,1,256]{2,1,0:T(1,128)S(1)} %bitcast.249), channel_id=4, replica_groups=mesh['tgt'=8,'src'=4] {'tgt'}, dimensions={0}, use_global_device_ids=true | all-gather | bytes 9216 | tf_op jit(solution)/shard_map/all_gather | solution.py:90
  260.0 2.7 fusion.12
  264.4 15.5 %all-reduce = f32[256]{0:T(256)S(1)} all-reduce(f32[256]{0:T(256)S(1)} %dynamic-update-slice), channel_id=5, replica_groups=mesh['tgt'=8,'src'=4] {'tgt'}, use_global_device_ids=true, to_apply=%add | all-reduce | flops 256 | bytes 2048
  281.5 2.2 convolution_bitcast_fusion.1
  283.8 8.4 %all_gather.29 = f32[4,32,256]{2,1,0:T(8,128)S(1)} all-gather(f32[1,32,256]{2,1,0:T(8,128)S(1)} %copy-done.3), channel_id=1, replica_groups=mesh['tgt'=8,'src'=4] {'src'}, dimensions={0}, use_global_device_ids=true | all-gather | bytes 163840 | tf_op jit(solution)/shard_map/all_gather | solution.py:65
  292.6 8.9 %all-reduce.2 = f32[4,256]{1,0:T(4,128)S(1)} all-reduce(f32[4,256]{1,0:T(4,128)S(1)} %convolution_add_fusion.1), channel_id=8, replica_groups=mesh['tgt'=8,'src'=4] {'src'}, use_global_device_ids=true, to_apply=%region_7.8.clone | all-reduce | flops 1024 | bytes 8192
  303.5 8.6 %psum.86 = f32[]{:T(128)} all-reduce(f32[]{:T(128)} %multiply_reduce_fusion.4), channel_id=1, replica_groups=mesh['tgt'=8,'src'=4] {'src'}, use_global_device_ids=true, to_apply=%region_9.10 | all-reduce | flops 1 | bytes 8 | tf_op jit(solution)/shard_map/psum | solution.py:28
  312.1 14.2 %psum.87 = f32[]{:T(128)} all-reduce(f32[]{:T(128)} %psum.86), channel_id=1, replica_groups=mesh['tgt'=8,'src'=4] {'tgt'}, use_global_device_ids=true, to_apply=%region_10.11 | all-reduce | flops 1 | bytes 8 | tf_op jit(solution)/shard_map/psum | solution.py:28
  327.6 9.6 %psum.88 = f32[]{:T(128)} all-reduce(f32[]{:T(128)} %multiply_reduce_fusion.3), channel_id=1, replica_groups=mesh['tgt'=8,'src'=4] {'src'}, use_global_device_ids=true, to_apply=%region_12.13 | all-reduce | flops 1 | bytes 8 | tf_op jit(solution)/shard_map/psum | solution.py:28
  337.2 14.3 %psum.89 = f32[]{:T(128)} all-reduce(f32[]{:T(128)} %psum.88), channel_id=1, replica_groups=mesh['tgt'=8,'src'=4] {'tgt'}, use_global_device_ids=true, to_apply=%region_13.14 | all-reduce | flops 1 | bytes 8 | tf_op jit(solution)/shard_map/psum | solution.py:28
  354.5 8.4 %all-gather.7 = f32[8,1,256]{2,1,0:T(1,128)S(1)} all-gather(f32[1,1,256]{2,1,0:T(1,128)S(1)} %bitcast.172), channel_id=6, replica_groups=mesh['tgt'=8,'src'=4] {'tgt'}, dimensions={0}, use_global_device_ids=true | all-gather | bytes 9216 | tf_op jit(solution)/shard_map/all_gather | solution.py:90
  363.5 2.7 fusion.10
  366.6 15.5 %all-reduce.1 = f32[256]{0:T(256)S(1)} all-reduce(f32[256]{0:T(256)S(1)} %dynamic-update-slice.1), channel_id=7, replica_groups=mesh['tgt'=8,'src'=4] {'tgt'}, use_global_device_ids=true, to_apply=%add.1 | all-reduce | flops 256 | bytes 2048
  382.2 2.2 convolution_bitcast_fusion
  384.9 8.9 %all-reduce.3 = f32[4,256]{1,0:T(4,128)S(1)} all-reduce(f32[4,256]{1,0:T(4,128)S(1)} %convolution_add_fusion), channel_id=9, replica_groups=mesh['tgt'=8,'src'=4] {'src'}, use_global_device_ids=true, to_apply=%region_14.15.clone | all-reduce | flops 1024 | bytes 8192
  395.1 9.5 %psum.90 = f32[]{:T(128)} all-reduce(f32[]{:T(128)} %multiply_reduce_fusion.2), channel_id=1, replica_groups=mesh['tgt'=8,'src'=4] {'src'}, use_global_device_ids=true, to_apply=%region_16.17 | all-reduce | flops 1 | bytes 8 | tf_op jit(solution)/shard_map/psum | solution.py:28
  404.6 14.2 %psum.91 = f32[]{:T(128)} all-reduce(f32[]{:T(128)} %psum.90), channel_id=1, replica_groups=mesh['tgt'=8,'src'=4] {'tgt'}, use_global_device_ids=true, to_apply=%region_17.18 | all-reduce | flops 1 | bytes 8 | tf_op jit(solution)/shard_map/psum | solution.py:28
  420.1 8.8 %psum.92 = f32[]{:T(128)} all-reduce(f32[]{:T(128)} %multiply_reduce_fusion.1), channel_id=1, replica_groups=mesh['tgt'=8,'src'=4] {'src'}, use_global_device_ids=true, to_apply=%region_19.20 | all-reduce | flops 1 | bytes 8 | tf_op jit(solution)/shard_map/psum | solution.py:28
  428.9 14.3 %psum.93 = f32[]{:T(128)} all-reduce(f32[]{:T(128)} %psum.92), channel_id=1, replica_groups=mesh['tgt'=8,'src'=4] {'tgt'}, use_global_device_ids=true, to_apply=%region_20.21 | all-reduce | flops 1 | bytes 8 | tf_op jit(solution)/shard_map/psum | solution.py:28
  444.6 1.9 multiply_reduce_fusion
  446.5 9.4 %psum.94 = f32[]{:T(128)} all-reduce(f32[]{:T(128)} %multiply_reduce_fusion), channel_id=1, replica_groups=mesh['tgt'=8,'src'=4] {'src'}, use_global_device_ids=true, to_apply=%region_22.23 | all-reduce | flops 1 | bytes 8 | tf_op jit(solution)/shard_map/psum | solution.py:28
  455.9 14.2 %psum.95 = f32[]{:T(128)} all-reduce(f32[]{:T(128)} %psum.94), channel_id=1, replica_groups=mesh['tgt'=8,'src'=4] {'tgt'}, use_global_device_ids=true, to_apply=%region_23.24 | all-reduce | flops 1 | bytes 8 | tf_op jit(solution)/shard_map/psum | solution.py:28
  (123 shorter events, 37.5 us)
Async XLA Ops:
  0.0 262.8 %copy-start = (f32[1,32,256]{2,1,0:T(8,128)S(1)}, f32[1,32,256]{2,1,0:T(8,128)}, u32[]{:S(2)}) copy-start(f32[1,32,256]{2,1,0:T(8,128)} %param.20) | copy-start | bytes 98308
  43.2 71.9 %copy-start.2 = (f32[256]{0:T(256)S(1)}, f32[256]{0:T(256)}, u32[]{:S(2)}) copy-start(f32[256]{0:T(256)} %param.13) | copy-start | bytes 3076
  43.2 216.2 %copy-start.4 = (s32[2,12]{1,0:T(2,128)S(1)}, s32[2,12]{1,0:T(2,128)}, u32[]{:S(2)}) copy-start(s32[2,12]{1,0:T(2,128)} %param.17) | copy-start | bytes 292
  115.1 147.8 %copy-start.6 = (u32[32]{0:T(128)S(1)}, u32[32]{0:T(128)}, u32[]{:S(2)}) copy-start(u32[32]{0:T(128)} %constant.65) | copy-start | bytes 388
  115.1 164.9 %copy-start.1 = (f32[1,4,8,1,1024]{4,3,2,1,0:T(1,128)S(1)}, f32[1,4,8,1,1024]{4,3,2,1,0:T(1,128)}, u32[]{:S(2)}) copy-start(f32[1,4,8,1,1024]{4,3,2,1,0:T(1,128)} %param.21) | copy-start | bytes 393220
  115.1 168.7 %copy-start.3 = (f32[1,32,256]{2,1,0:T(8,128)S(1)}, f32[1,32,256]{2,1,0:T(8,128)}, u32[]{:S(2)}) copy-start(f32[1,32,256]{2,1,0:T(8,128)} %param.19) | copy-start | bytes 98308
  115.1 186.4 %copy-start.5 = (u32[32]{0:T(128)S(1)}, u32[32]{0:T(128)}, u32[]{:S(2)}) copy-start(u32[32]{0:T(128)} %constant.77) | copy-start | bytes 388
